TPU v7x, 32 devices: a whole 2x2x4 slice. The times are simulated.
32 devices in a mesh: mem: 4 (over z), lat: 2 (over x), lon: 4 (over y, core).
Axes of the slice: x: 2, y: 2, z: 4, core: 2. Of those that a mesh axis runs over, the one named last changes fastest.
Arguments:
- members: bfloat16 [8, 16, 128, 512], P('mem', None, 'lon', 'lat'), may hold values from -6 to 6
- control_fine: bfloat16 [8, 16, 128, 512], P('mem', None, 'lon', 'lat'), may hold values from -6 to 6
- control_mid: bfloat16 [8, 16, 64, 256], P('mem', None, 'lon', 'lat'), may hold values from -6 to 6
- control_coarse: bfloat16 [8, 16, 32, 128], P('mem', None, 'lon', 'lat'), may hold values from -6 to 6
- vertical: bfloat16 [3, 16, 16], replicated, may hold values from 0 to 0.25
- mid_picks: int32 [320], replicated, may hold values from 0 to 1
- coarse_picks: int32 [160], replicated, may hold values from 0 to 3
- band_radii: int32 [3], replicated, may hold values from 4 to 8
Outputs:
- increment: float32 [4, 512, 512], P('lon', 'mem', 'lat')
Inputs may be any that keep to these rules, and one draw needn't show every extreme that they name: `mid_picks`: entry i of the first 256 entries picks fine row 2 i + entry for middle-band row i; entry j of the rest picks fine column 2 j + entry for middle-band column j. `coarse_picks`: entry i of the first 128 entries picks fine row 4 i + entry for coarse-band row i; entry j of the rest picks fine column 4 j + entry for coarse-band column j. `band_radii`: radius of each band's horizontal taper, in that band's cells.
All inputs are finite; a program needn't handle non-finite values.
Results may differ from a plain program's by a relative error of at most 0.0062.
Values may be sent and summed in bfloat16 or wider, within the bound.
A program may use at most 64 MiB of HBM per device.

v0:
```python
import math

import jax
import jax.numpy as jnp
from jax import lax
from jax.sharding import PartitionSpec as P

REACH = 8


band_factors = (1, 2, 4)


def extended(cells, sides, width, closed):
    for axis, dim in sides:
        count = lax.axis_size(axis)
        ends = count if closed else count - 1
        head = lax.slice_in_dim(cells, 0, width, axis=dim)
        tail = lax.slice_in_dim(cells, cells.shape[dim] - width, cells.shape[dim], axis=dim)
        cells = jnp.concatenate(
            [
                lax.ppermute(tail, axis, [(i, (i + 1) % count) for i in range(ends)]),
                cells,
                lax.ppermute(head, axis, [((i + 1) % count, i) for i in range(ends)]),
            ],
            axis=dim,
        )
    return cells


def tap_weights(radius):
    offsets = jnp.arange(-REACH, REACH + 1).astype(jnp.float32)
    reach_now = radius.astype(jnp.float32)
    spread = 0.5 * reach_now
    unnormed = jnp.where(
        jnp.abs(offsets) <= reach_now,
        jnp.exp(-0.5 * jnp.square(offsets / spread)),
        jnp.float32(0.0),
    )
    return (unnormed / jnp.sum(unnormed)).astype(jnp.bfloat16)


def band_matrix(weights, out_length, in_length, start):
    offset = (
        jnp.arange(in_length, dtype=jnp.int32)[None, :]
        - jnp.arange(out_length, dtype=jnp.int32)[:, None]
        - start
        - REACH
    )
    weight_wide = weights.astype(jnp.float32)
    matrix = jnp.zeros((out_length, in_length), jnp.float32)
    for tap_index in range(2 * REACH + 1):
        matrix = matrix + jnp.where(
            offset == tap_index - REACH, weight_wide[tap_index], jnp.float32(0.0)
        )
    return matrix.astype(jnp.bfloat16)


def vertical_mix(vertical_band, control):
    return jnp.einsum(
        "kl,mlcr->mkcr", vertical_band, control, preferred_element_type=jnp.float32
    ).astype(jnp.bfloat16)


def rim_filter(mixed, weights):
    col_count = mixed.shape[2]
    row_count = mixed.shape[3]
    rimmed = extended(mixed, (("lat", 3),), REACH, False)
    row_matrix = band_matrix(weights, row_count, row_count + 2 * REACH, 0)
    across = jnp.einsum(
        "mkcj,ij->mkci", rimmed, row_matrix, preferred_element_type=jnp.float32
    ).astype(jnp.bfloat16)
    wrapped = extended(across, (("lon", 2),), REACH, True)
    col_matrix = band_matrix(weights, col_count, col_count + 2 * REACH, 0)
    return jnp.einsum("cj,mkjr->mkcr", col_matrix, wrapped, preferred_element_type=jnp.float32)


def whole_filter(mixed, weights):
    own_cols = mixed.shape[2]
    own_rows = mixed.shape[3]
    gathered = lax.all_gather(mixed, "lat", axis=3, tiled=True)
    gathered = lax.all_gather(gathered, "lon", axis=2, tiled=True)
    total_cols = gathered.shape[2]
    total_rows = gathered.shape[3]
    padded = jnp.pad(gathered, ((0, 0), (0, 0), (0, 0), (REACH, REACH)))
    row_start = lax.axis_index("lat") * own_rows
    row_matrix = band_matrix(weights, own_rows, total_rows + 2 * REACH, row_start)
    across = jnp.einsum(
        "mkcj,ij->mkci", padded, row_matrix, preferred_element_type=jnp.float32
    ).astype(jnp.bfloat16)
    wrapped = jnp.concatenate(
        [across[:, :, total_cols - REACH :, :], across, across[:, :, :REACH, :]], axis=2
    )
    col_start = lax.axis_index("lon") * own_cols
    col_matrix = band_matrix(weights, own_cols, total_cols + 2 * REACH, col_start)
    return jnp.einsum("cj,mkjr->mkcr", col_matrix, wrapped, preferred_element_type=jnp.float32)


def picker(chosen, factor):
    length = chosen.shape[0]
    target = factor * jnp.arange(length, dtype=jnp.int32)[:, None] + chosen[:, None]
    return (target == jnp.arange(length * factor, dtype=jnp.int32)[None, :]).astype(jnp.bfloat16)


def restrict(members, chosen, factor):
    band_cols = members.shape[2] // factor
    band_rows = members.shape[3] // factor
    row_start = lax.axis_index("lat") * band_rows
    col_start = band_rows * lax.axis_size("lat") + lax.axis_index("lon") * band_cols
    row_pick = picker(lax.dynamic_slice_in_dim(chosen, row_start, band_rows), factor)
    col_pick = picker(lax.dynamic_slice_in_dim(chosen, col_start, band_cols), factor)
    by_rows = jnp.einsum(
        "mkcr,ir->mkci", members, row_pick, preferred_element_type=jnp.float32
    ).astype(jnp.bfloat16)
    return jnp.einsum(
        "jc,mkci->mkji", col_pick, by_rows, preferred_element_type=jnp.float32
    ).astype(jnp.bfloat16)


def on_device(
    members,
    control_fine,
    control_mid,
    control_coarse,
    vertical,
    mid_picks,
    coarse_picks,
    band_radii,
):
    member_total = members.shape[0] * lax.axis_size("mem")
    controls = (control_fine, control_mid, control_coarse)
    chosen_all = (None, mid_picks, coarse_picks)
    filtered_bands = []
    for band_index in range(2):
        weights = tap_weights(band_radii[band_index])
        mixed = vertical_mix(vertical[band_index], controls[band_index])
        filtered_bands.append(rim_filter(mixed, weights))
    coarse_weights = tap_weights(band_radii[2])
    coarse_mixed = vertical_mix(vertical[2], control_coarse)
    filtered_bands.append(whole_filter(coarse_mixed, coarse_weights))
    member_sums = []
    for band_index in range(3):
        factor = band_factors[band_index]
        restricted = members if factor == 1 else restrict(members, chosen_all[band_index], factor)
        product = restricted.astype(jnp.float32) * filtered_bands[band_index]
        member_sums.append(jnp.sum(product, axis=0))
    accumulated = None
    for band_index in range(3):
        factor = band_factors[band_index]
        summed = member_sums[band_index]
        flat = summed.reshape(summed.shape[0] * summed.shape[1], summed.shape[2])
        reduced = lax.psum_scatter(flat, "mem", scatter_dimension=0, tiled=True)
        spread_out = jnp.repeat(jnp.repeat(reduced, factor, axis=0), factor, axis=1)
        accumulated = spread_out if accumulated is None else accumulated + spread_out
    increment = accumulated / math.sqrt(member_total - 1)
    return increment[None, :, :]


def solution(mesh):
    placed = (
        P("mem", None, "lon", "lat"),
        P("mem", None, "lon", "lat"),
        P("mem", None, "lon", "lat"),
        P("mem", None, "lon", "lat"),
        P(),
        P(),
        P(),
        P(),
    )
    return jax.shard_map(
        on_device, mesh=mesh, in_specs=placed, out_specs=P("lon", "mem", "lat"), check_vma=False
    )
```

profile of v0, /device:TPU:0, one launch (start us, length us, event | category | flops | bytes accessed | tf_op | source)
XLA Modules:
  0.0 157.8 jit_solution(10954879942256354719)
XLA Ops:
  6.5 0.8 dynamic-slice_add_fusion.1
  7.4 0.8 dynamic-slice_add_fusion
  8.1 1.0 fusion.14
  9.1 0.3 copy.35
  9.4 9.9 %all_gather.6 = bf16[2,16,8,128]{1,2,0,3:T(8,128)(2,1)S(1)} all-gather(bf16[2,16,8,64]{1,2,0,3:T(8,128)(2,1)S(1)} %copy.35), channel_id=1, replica_groups=mesh['mem'=4,'lat'=2,'lon'=4] {'lat'}, dimensions={3}, use_global_device_ids=true | all-gather | bytes 98304 | tf_op jit(solution)/shard_map/all_gather | solution.py:81
  19.3 0.4 copy.36
  19.8 6.1 %all_gather.7 = bf16[2,16,32,128]{3,2,1,0:T(8,128)(2,1)S(1)} all-gather(bf16[2,16,8,128]{3,2,1,0:T(8,128)(2,1)S(1)} %copy.36), channel_id=1, replica_groups=mesh['mem'=4,'lat'=2,'lon'=4] {'lon'}, dimensions={2}, use_global_device_ids=true | all-gather | bytes 327680 | tf_op jit(solution)/shard_map/all_gather | solution.py:82
  25.8 0.6 fusion.511
  27.0 0.6 fusion.392
  27.6 0.6 convert_convert_fusion
  28.2 0.7 fusion.513
  28.9 11.0 %convolution_convert_fusion.2 = bf16[2,16,32,64]{3,2,1,0:T(8,128)(2,1)S(1)} fusion(bf16[2,16,32,128]{3,2,1,0:T(8,128)(2,1)S(1)} %all_gather.7, f32[]{:T(128)} %bitcast.89, f32[]{:T(128)} %bitcast.88, f32[]{:T(128)} %bitcast.87, f32[]{:T(128)} %bitcast.86, f32[]{:T(128)} %bitcast.85, f32[]{:T(128)} %bitcast.84, f32[]{:T(128)} %bitcast.83, f32[]{:T(128)} %bitcast.82, ...), kind=kOutput, calls=%fused_computation.6 | convolution fusion | flops 19437568 | bytes 393288 | tf_op jit(solution)/shard_map/mkcj,ij->mkci/dot_general | solution.py:88
  40.0 0.5 fusion.13
  40.5 11.4 %fusion.11 = f32[16,64,8]{1,2,0:T(8,128)} fusion(f32[2,16,64,8]{2,3,1,0:T(8,128)S(1)} %fusion.13, bf16[2,16,8,64]{3,2,1,0:T(8,128)(2,1)S(1)} %get-tuple-element.10, bf16[2,16,32,64]{3,2,1,0:T(8,128)(2,1)S(1)} %convolution_convert_fusion.2, bf16[2,16,8,64]{3,2,1,0:T(8,128)(2,1)S(1)} %get-tuple-element.9, f32[]{:T(128)} %bitcast.89, f32[]{:T(128)} %bitcast.88, ...), kind=kOutput, calls=%fused_computation.21 | convolution fusion | flops 2208000 | bytes 294984 | tf_op jit(solution)/shard_map/cj,mkjr->mkcr/dot_general | solution.py:96
  52.0 0.4 fusion.2
  52.4 0.1 fusion.506
  52.5 1.3 collective-permute-start.1
  53.8 4.6 %collective-permute-start = (bf16[2,16,32,8]{3,1,2,0:T(8,128)(2,1)S(1)}, bf16[2,16,32,8]{3,1,2,0:T(8,128)(2,1)S(1)}, u32[]{:S(2)}, u32[]{:S(2)}) collective-permute-start(bf16[2,16,32,8]{3,1,2,0:T(8,128)(2,1)S(1)} %get-tuple-element.7), channel_id=1, source_target_pairs={{0,4},{1,5},{2,6},{3,7},{8,12},{9,13},{10,14},{11,15},{16,20},{17,... | collective-permute-start | bytes 49160 | tf_op jit(solution)/shard_map/ppermute | solution.py:22
  58.4 0.2 fusion.10
  58.6 0.1 fusion.509
  58.7 1.3 collective-permute-start.5
  60.0 4.6 %collective-permute-start.4 = (bf16[2,16,16,8]{3,1,2,0:T(8,128)(2,1)S(1)}, bf16[2,16,16,8]{3,1,2,0:T(8,128)(2,1)S(1)}, u32[]{:S(2)}, u32[]{:S(2)}) collective-permute-start(bf16[2,16,16,8]{3,1,2,0:T(8,128)(2,1)S(1)} %get-tuple-element.13), channel_id=1, source_target_pairs={{0,4},{1,5},{2,6},{3,7},{8,12},{9,13},{10,14},{11,15},{16,20},{17,... | collective-permute-start | bytes 24584 | tf_op jit(solution)/shard_map/ppermute | solution.py:22
  65.2 0.6 fusion.390
  65.9 0.6 convert_convert_fusion.2
  66.5 0.7 fusion.512
  67.2 0.1 dynamic-slice_add_fusion.3
  67.3 0.1 dynamic-slice_add_fusion.2
  68.0 0.6 fusion.391
  68.6 0.7 convert_convert_fusion.1
  69.3 0.5 fusion.9
  69.9 0.7 fusion.510
  70.6 0.2 pad_maximum_fusion.1
  70.8 10.9 %convolution_convert_fusion.6 = bf16[2,16,16,128]{3,2,1,0:T(8,128)(2,1)S(1)} fusion(bf16[2,16,16,144]{3,1,2,0:T(8,128)(2,1)S(1)} %pad_maximum_fusion.1, f32[]{:T(128)} %bitcast.54, f32[]{:T(128)} %bitcast.53, f32[]{:T(128)} %bitcast.52, f32[]{:T(128)} %bitcast.51, f32[]{:T(128)} %bitcast.50, f32[]{:T(128)} %bitcast.49, f32[]{:T(128)} %bitcast.48, ...), kind=kOutput, calls=%fused_computation.16 | convolution fusion | flops 19916800 | bytes 278596 | tf_op jit(solution)/shard_map/mkcj,ij->mkci/dot_general | solution.py:70
  81.8 0.4 collective-permute-start.7
  82.1 0.2 collective-permute-start.6
  82.3 0.5 pad_maximum_fusion
  82.8 11.2 %convolution_convert_fusion = bf16[2,16,32,256]{3,2,1,0:T(8,128)(2,1)S(1)} fusion(bf16[2,16,32,272]{3,1,2,0:T(8,128)(2,1)S(1)} %pad_maximum_fusion, f32[]{:T(128)} %bitcast.21, f32[]{:T(128)} %bitcast.20, f32[]{:T(128)} %bitcast.19, f32[]{:T(128)} %bitcast.18, f32[]{:T(128)} %bitcast.17, f32[]{:T(128)} %bitcast.16, f32[]{:T(128)} %bitcast.15, f32[]{:T(128)} %bitcast.14, ...), kind=kOutput, calls=%fused_computation.2 | convolution fusion | flops 146558976 | bytes 1081412 | tf_op jit(solution)/shard_map/mkcj,ij->mkci/dot_general | solution.py:70
  94.0 1.6 %collective-permute-start.3 = (bf16[2,16,8,256]{3,2,1,0:T(8,128)(2,1)S(1)}, bf16[2,16,8,256]{3,2,1,0:T(8,128)(2,1)S(1)}, u32[]{:S(2)}, u32[]{:S(2)}) collective-permute-start(bf16[2,16,8,256]{3,2,1,0:T(8,128)(2,1)S(1)} %get-tuple-element.6), channel_id=1, source_target_pairs={{1,0},{2,1},{3,2},{0,3},{5,4},{6,5},{7,6},{4,7},{9,8},{10,9},{11,1... | collective-permute-start | bytes 393224 | tf_op jit(solution)/shard_map/ppermute | solution.py:24
  95.7 11.5 %fusion.7 = f32[16,128,16]{1,2,0:T(8,128)} fusion(f32[2,16,128,16]{2,3,1,0:T(8,128)S(1)} %fusion.9, bf16[2,16,8,128]{3,2,1,0:T(8,128)(2,1)S(1)} %collective-permute-done.7, bf16[2,16,16,128]{3,2,1,0:T(8,128)(2,1)S(1)} %convolution_convert_fusion.6, bf16[2,16,8,128]{3,2,1,0:T(8,128)(2,1)S(1)} %collective-permute-done.6, f32[]{:T(128)} %bitcast.54, ...), kind=kOutput, calls=%fused_computation.14 | convolution fusion | flops 5106176 | bytes 655428 | tf_op jit(solution)/shard_map/cj,mkjr->mkcr/dot_general | solution.py:75
  107.2 11.6 %fusion.1 = f32[16,32,256]{2,1,0:T(8,128)} fusion(bf16[2,16,32,256]{3,2,1,0:T(8,128)(2,1)S(1)} %copy-done.1, bf16[2,16,8,256]{3,2,1,0:T(8,128)(2,1)S(1)} %collective-permute-done.3, bf16[2,16,32,256]{3,2,1,0:T(8,128)(2,1)S(1)} %convolution_convert_fusion, bf16[2,16,8,256]{3,2,1,0:T(8,128)(2,1)S(1)} %collective-permute-done.2, f32[]{:T(128)} %bitcast.21, ...), kind=kOutput, calls=%fused_computation.4 | convolution fusion | flops 28261888 | bytes 1835076 | tf_op jit(solution)/shard_map/cj,mkjr->mkcr/dot_general | solution.py:75
  118.9 0.7 broadcast_in_dim.588
  119.7 0.1 copy.38
  119.8 7.5 %reduce-scatter.6.cloned.1.call-done = f32[64,128]{1,0:T(8,128)} async-done(((f32[256,128]{1,0:T(8,128)}), f32[64,128]{1,0:T(8,128)}) %reduce-scatter.6.cloned.1.call-update) | async-done | bytes 32784 | tf_op jit(solution)/shard_map/reduce_scatter | solution.py:152
  127.3 0.8 broadcast_in_dim.550
  128.1 0.1 copy.32
  128.3 0.1 copy.33
  128.4 21.3 %reduce-scatter.4.cloned.1.call-done = f32[128,256]{1,0:T(8,128)} async-done(((f32[512,256]{1,0:T(8,128)}), f32[128,256]{1,0:T(8,128)}) %reduce-scatter.4.cloned.1.call-update) | async-done | bytes 131088 | tf_op jit(solution)/shard_map/reduce_scatter | solution.py:152
  149.7 1.6 %multiply_bitcast_fusion = f32[1,128,256]{2,1,0:T(8,128)} fusion(f32[128,256]{1,0:T(8,128)S(1)} %copy.38, f32[128,256]{1,0:T(8,128)} %reduce-scatter.4.cloned.1.call-done, f32[128,256]{1,0:T(8,128)S(1)} %copy.33), kind=kLoop, calls=%fused_computation.103 | loop fusion | flops 98304 | bytes 524288 | tf_op jit(solution)/shard_map/broadcast_in_dim | solution.py:156
  (34 shorter events, 0.4 us)
Async XLA Ops:
  6.5 45.4 %copy-start = (bf16[2,16,32,256]{3,2,1,0:T(8,128)(2,1)S(1)}, bf16[2,16,32,256]{3,2,1,0:T(8,128)(2,1)}, u32[]{:S(2)}) copy-start(bf16[2,16,32,256]{3,2,1,0:T(8,128)(2,1)} %param.9) | copy-start | bytes 1572868
  6.5 112.4 %reduce-scatter.8.cloned.1.call-start = ((), (), s32[]{:S(2)}) async-start(), calls=%async_computation.5 | async-start | bytes 81920 | tf_op jit(solution)/shard_map/reduce_scatter | solution.py:152
  9.4 16.5 %copy-start.4 = (s32[3]{0:T(128)S(1)}, s32[3]{0:T(128)}, u32[]{:S(2)}) copy-start(s32[3]{0:T(128)} %param.15) | copy-start | bytes 40
  28.9 11.1 %copy-start.1 = (bf16[2,16,32,256]{3,2,1,0:T(8,128)(2,1)S(1)}, bf16[2,16,32,256]{3,2,1,0:T(8,128)(2,1)}, u32[]{:S(2)}) copy-start(bf16[2,16,32,256]{3,2,1,0:T(8,128)(2,1)} %param.8) | copy-start | bytes 1572868
  40.0 12.0 %copy-start.3 = (bf16[3,16,16]{2,1,0:T(8,128)(2,1)S(1)}, bf16[3,16,16]{2,1,0:T(8,128)(2,1)}, u32[]{:S(2)}) copy-start(bf16[3,16,16]{2,1,0:T(8,128)(2,1)} %param.12) | copy-start | bytes 4612
  51.9 75.4 %reduce-scatter.6.cloned.1.call-start = ((), (), s32[]{:S(2)}) async-start(), calls=%async_computation.4 | async-start | bytes 163840 | tf_op jit(solution)/shard_map/reduce_scatter | solution.py:152
  52.4 6.1 %copy-start.2 = (bf16[2,16,16,128]{3,2,1,0:T(8,128)(2,1)S(1)}, bf16[2,16,16,128]{3,2,1,0:T(8,128)(2,1)}, u32[]{:S(2)}) copy-start(bf16[2,16,16,128]{3,2,1,0:T(8,128)(2,1)} %param.10) | copy-start | bytes 393220
  52.4 14.8 %copy-start.5 = (s32[320]{0:T(512)S(1)}, s32[320]{0:T(512)}, u32[]{:S(2)}) copy-start(s32[320]{0:T(512)} %param.13) | copy-start | bytes 3844
  52.5 29.8 %collective-permute-start.1 = (bf16[2,16,32,8]{3,1,2,0:T(8,128)(2,1)S(1)}, bf16[2,16,32,8]{3,1,2,0:T(8,128)(2,1)S(1)}, u32[]{:S(2)}, u32[]{:S(2)}) collective-permute-start(bf16[2,16,32,8]{3,1,2,0:T(8,128)(2,1)S(1)} %get-tuple-element.8), channel_id=1, source_target_pairs={{4,0},{5,1},{6,2},{7,3},{12,8},{13,9},{14,10},{15,11},{20,16},{21,... | collective-permute-start | bytes 49160 | tf_op jit(solution)/shard_map/ppermute | solution.py:24
  53.8 28.5 %collective-permute-start = (bf16[2,16,32,8]{3,1,2,0:T(8,128)(2,1)S(1)}, bf16[2,16,32,8]{3,1,2,0:T(8,128)(2,1)S(1)}, u32[]{:S(2)}, u32[]{:S(2)}) collective-permute-start(bf16[2,16,32,8]{3,1,2,0:T(8,128)(2,1)S(1)} %get-tuple-element.7), channel_id=1, source_target_pairs={{0,4},{1,5},{2,6},{3,7},{8,12},{9,13},{10,14},{11,15},{16,20},{17,... | collective-permute-start | bytes 49160 | tf_op jit(solution)/shard_map/ppermute | solution.py:22
  58.7 11.9 %collective-permute-start.5 = (bf16[2,16,16,8]{3,1,2,0:T(8,128)(2,1)S(1)}, bf16[2,16,16,8]{3,1,2,0:T(8,128)(2,1)S(1)}, u32[]{:S(2)}, u32[]{:S(2)}) collective-permute-start(bf16[2,16,16,8]{3,1,2,0:T(8,128)(2,1)S(1)} %get-tuple-element.14), channel_id=1, source_target_pairs={{4,0},{5,1},{6,2},{7,3},{12,8},{13,9},{14,10},{15,11},{20,16},{21,... | collective-permute-start | bytes 24584 | tf_op jit(solution)/shard_map/ppermute | solution.py:24
  60.0 10.6 %collective-permute-start.4 = (bf16[2,16,16,8]{3,1,2,0:T(8,128)(2,1)S(1)}, bf16[2,16,16,8]{3,1,2,0:T(8,128)(2,1)S(1)}, u32[]{:S(2)}, u32[]{:S(2)}) collective-permute-start(bf16[2,16,16,8]{3,1,2,0:T(8,128)(2,1)S(1)} %get-tuple-element.13), channel_id=1, source_target_pairs={{0,4},{1,5},{2,6},{3,7},{8,12},{9,13},{10,14},{11,15},{16,20},{17,... | collective-permute-start | bytes 24584 | tf_op jit(solution)/shard_map/ppermute | solution.py:22
  81.8 13.9 %collective-permute-start.7 = (bf16[2,16,8,128]{3,2,1,0:T(8,128)(2,1)S(1)}, bf16[2,16,8,128]{3,2,1,0:T(8,128)(2,1)S(1)}, u32[]{:S(2)}, u32[]{:S(2)}) collective-permute-start(bf16[2,16,8,128]{3,2,1,0:T(8,128)(2,1)S(1)} %get-tuple-element.12), channel_id=1, source_target_pairs={{1,0},{2,1},{3,2},{0,3},{5,4},{6,5},{7,6},{4,7},{9,8},{10,9},{11,1... | collective-permute-start | bytes 196616 | tf_op jit(solution)/shard_map/ppermute | solution.py:24
  82.1 13.5 %collective-permute-start.6 = (bf16[2,16,8,128]{3,2,1,0:T(8,128)(2,1)S(1)}, bf16[2,16,8,128]{3,2,1,0:T(8,128)(2,1)S(1)}, u32[]{:S(2)}, u32[]{:S(2)}) collective-permute-start(bf16[2,16,8,128]{3,2,1,0:T(8,128)(2,1)S(1)} %get-tuple-element.11), channel_id=1, source_target_pairs={{0,1},{1,2},{2,3},{3,0},{4,5},{5,6},{6,7},{7,4},{8,9},{9,10},{10,1... | collective-permute-start | bytes 196616 | tf_op jit(solution)/shard_map/ppermute | solution.py:22
  94.0 13.2 %collective-permute-start.3 = (bf16[2,16,8,256]{3,2,1,0:T(8,128)(2,1)S(1)}, bf16[2,16,8,256]{3,2,1,0:T(8,128)(2,1)S(1)}, u32[]{:S(2)}, u32[]{:S(2)}) collective-permute-start(bf16[2,16,8,256]{3,2,1,0:T(8,128)(2,1)S(1)} %get-tuple-element.6), channel_id=1, source_target_pairs={{1,0},{2,1},{3,2},{0,3},{5,4},{6,5},{7,6},{4,7},{9,8},{10,9},{11,1... | collective-permute-start | bytes 393224 | tf_op jit(solution)/shard_map/ppermute | solution.py:24
  95.6 11.6 %collective-permute-start.2 = (bf16[2,16,8,256]{3,2,1,0:T(8,128)(2,1)S(1)}, bf16[2,16,8,256]{3,2,1,0:T(8,128)(2,1)S(1)}, u32[]{:S(2)}, u32[]{:S(2)}) collective-permute-start(bf16[2,16,8,256]{3,2,1,0:T(8,128)(2,1)S(1)} %get-tuple-element.5), channel_id=1, source_target_pairs={{0,1},{1,2},{2,3},{3,0},{4,5},{5,6},{6,7},{7,4},{8,9},{9,10},{10,1... | collective-permute-start | bytes 393224 | tf_op jit(solution)/shard_map/ppermute | solution.py:22
  107.1 42.5 %reduce-scatter.4.cloned.1.call-start = ((), (), s32[]{:S(2)}) async-start(), calls=%async_computation.3 | async-start | bytes 655360 | tf_op jit(solution)/shard_map/reduce_scatter | solution.py:152
Sparse Core Ops, SparseCore 0:
  52.0 20.4 reduce-scatter.7
  107.3 20.0 reduce-scatter.5
  129.6 20.0 reduce-scatter.3
where the time goes:
time: 159 us; the launch traced here: 158 us
  matrix products  70.2 us (44%)
  waiting for transfers between devices  28.9 us (18%)
  blocking collectives  16 us (10%)
  between operations  15.3 us (10%)
  starting transfers between devices  14 us (9%)
  other arithmetic  7.71 us (5%)
  local copies, waits for them, and re-layouts  5.74 us (4%)
    reduce_scatter x3, waiting for transfers between devices, on_device(): reduced = lax.psum_scatter(flat, 'mem', scatter_dimension=0, tiled=True)  28.8 us
    dot_general x2, matrix products, rim_filter(): jnp.einsum('cj,mkjr->mkcr', col_matrix, wrapped, preferred_element_type=j...  23.1 us
    dot_general x2, matrix products, rim_filter(): jnp.einsum('mkcj,ij->mkci', rimmed, row_matrix, preferred_element_type=jn...  22.1 us
    dot_general x1, matrix products, whole_filter(): jnp.einsum('cj,mkjr->mkcr', col_matrix, wrapped, preferred_element_type=j...  11.4 us
    dot_general x1, matrix products, whole_filter(): jnp.einsum('mkcj,ij->mkci', padded, row_matrix, preferred_element_type=jn...  11 us
    all_gather x1, blocking collectives, whole_filter(): gathered = lax.all_gather(mixed, 'lat', axis=3, tiled=True)  9.94 us
    ppermute x4, starting transfers between devices, extended(): lax.ppermute(tail, axis, [(i, (i + 1) % count) for i in range(ends)])  9.31 us
    all_gather x1, blocking collectives, whole_filter(): gathered = lax.all_gather(gathered, 'lon', axis=2, tiled=True)  6.06 us
  transfers between devices with their start and end apart: 11, of which 2 were waited for; matrix products, arithmetic and copies ran while one was open for 34% of the time, Pallas kernels for 0%

commit v1 on v0

v1 whole, which is shorter than its diff:
```python
import functools
import math

import jax
import jax.numpy as jnp
from jax import lax
from jax.experimental import pallas as pl
from jax.experimental.pallas import tpu as pltpu
from jax.sharding import PartitionSpec as P

REACH = 8
FACTORS = (1, 2, 4)
MESH = pl.DeviceIdType.MESH
F32 = jnp.float32
BF16 = jnp.bfloat16


def log2(value):
    shift = value.bit_length() - 1
    assert value == 1 << shift
    return shift


def iota(shape, dim):
    return lax.broadcasted_iota(jnp.int32, shape, dim)


def dot(left, right):
    return jnp.dot(left, right, preferred_element_type=F32)


def dot_nt(left, right):
    return lax.dot_general(left, right, (((1,), (1,)), ((), ())), preferred_element_type=F32)


def dot_tn(left, right):
    return lax.dot_general(left, right, (((0,), (0,)), ((), ())), preferred_element_type=F32)


def one_hot(condition):
    return jnp.where(condition, 1.0, 0.0).astype(BF16)


def flat(cells):
    lanes = cells.shape[-1]
    if cells.shape[-2] % 16 == 0:
        return cells.reshape(-1, lanes)
    return cells.astype(F32).reshape(-1, lanes).astype(BF16)


def taper(radius, distance):
    reach_now = radius.astype(F32)
    spread = 0.5 * reach_now

    def raw(offset):
        offset = offset.astype(F32)
        return jnp.where(
            jnp.abs(offset) <= reach_now, jnp.exp(-0.5 * jnp.square(offset / spread)), 0.0
        )

    lane = iota((1, 128), 1)
    each = jnp.where(lane <= 2 * REACH, raw(lane - REACH), 0.0)
    total = jnp.sum(each, axis=1, keepdims=True)
    return raw(distance) / total


def pick_vector(picks_ref, start, rows, period):
    picks = picks_ref[...].astype(F32)
    length = picks.shape[1]
    place = iota((rows, length), 0)
    index = start + (place if period == rows else place & (period - 1))
    hit = iota((rows, length), 1) == index
    return jnp.sum(jnp.where(hit, picks, 0.0), axis=1, keepdims=True)


def kernel(
    sizes,
    members_hbm,
    fine_hbm,
    mid_hbm,
    coarse_hbm,
    vertical_ref,
    mid_picks_ref,
    coarse_picks_ref,
    radii_ref,
    out_ref,
    members_ref,
    own0,
    own1,
    own2,
    side0,
    side1,
    side2,
    strip_out,
    strip_in,
    corner_out,
    corner_in,
    field_ref,
    sum_out,
    sum_in,
    load_sem,
    lon_send,
    lon_recv,
    strip_send,
    strip_recv,
    corner_send,
    corner_recv,
    sum_send,
    sum_recv,
):
    n_mem, n_lat, n_lon, shifts = sizes
    mem, lat, lon = lax.axis_index("mem"), lax.axis_index("lat"), lax.axis_index("lon")
    count, levels, cols, rows = members_ref.shape
    controls_hbm = (fine_hbm, mid_hbm, coarse_hbm)
    owns = (own0, own1, own2)
    sides = (side0, side1, side2)
    band_cols = [cols // f for f in FACTORS]
    band_rows = [rows // f for f in FACTORS]
    after, before = lax.rem(lon + 1, n_lon), lax.rem(lon + n_lon - 1, n_lon)

    loads = [
        pltpu.make_async_copy(src, dst, load_sem.at[i])
        for i, (src, dst) in enumerate(zip(controls_hbm + (members_hbm,), owns + (members_ref,)))
    ]
    for load in loads:
        load.start()

    partners = [{"lon": before}, {"lon": after}]
    for s in shifts:
        there = lax.rem(lat + s, n_lat)
        partners += [{"lat": there}, {"lat": there, "lon": before}, {"lat": there, "lon": after}]
    for s in range(1, n_mem):
        partners.append({"mem": lax.rem(mem + s, n_mem)})
    barrier = pltpu.get_barrier_semaphore()
    for partner in partners:
        pl.semaphore_signal(barrier, inc=1, device_id=partner, device_id_type=MESH)
    pl.semaphore_wait(barrier, len(partners))

    def remote(src, dst, send, recv, device):
        return pltpu.make_async_remote_copy(
            src_ref=src, dst_ref=dst, send_sem=send, recv_sem=recv, device_id=device, device_id_type=MESH
        )

    lon_copies = []
    for b in range(3):
        width = band_cols[b]
        lon_copies.append(
            remote(
                controls_hbm[b].at[:, :, width - REACH : width, :],
                sides[b].at[:, 0],
                lon_send.at[2 * b],
                lon_recv.at[2 * b],
                {"lon": after},
            )
        )
        lon_copies.append(
            remote(
                controls_hbm[b].at[:, :, 0:REACH, :],
                sides[b].at[:, 1],
                lon_send.at[2 * b + 1],
                lon_recv.at[2 * b + 1],
                {"lon": before},
            )
        )
    for copy in lon_copies:
        copy.start()

    starts = []
    place = 0
    for b in range(3):
        starts.append(place)
        place += count * levels * band_cols[b]
    lat_copies = []
    for b in range(3):
        loads[b].wait()
    for b in range(3):
        length = band_rows[b]
        h = iota((2 * REACH, length), 0)
        i = iota((2 * REACH, length), 1)
        edge = one_hot(i == jnp.where(h < REACH, h, length - 2 * REACH + h))
        width = count * levels * band_cols[b]
        strip_out[:, starts[b] : starts[b] + width] = dot_nt(edge, flat(owns[b][...])).astype(BF16)
        near = owns[b][...].astype(F32)
        for side in range(2):
            first = 0 if side == 0 else band_cols[b] - REACH
            part = near[:, :, first : first + REACH, :].reshape(-1, length).astype(BF16)
            packed = dot_nt(edge, part).astype(BF16)
            for m in range(count):
                lanes = levels * REACH
                corner_out[side, b * count + m] = packed[:, m * lanes : (m + 1) * lanes]
    for k, s in enumerate(shifts):
        slot = shifts.index((n_lat - s) % n_lat)
        there = lax.rem(lat + s, n_lat)
        lat_copies.append(
            remote(strip_out, strip_in.at[slot], strip_send.at[slot], strip_recv.at[slot], {"lat": there})
        )
        for side in range(2):
            target = before if side == 0 else after
            lat_copies.append(
                remote(
                    corner_out.at[side],
                    corner_in.at[slot, :, 1 - side],
                    corner_send.at[2 * slot + side],
                    corner_recv.at[2 * slot + side],
                    {"lat": there, "lon": target},
                )
            )
    for copy in lat_copies:
        copy.start()

    row_own, row_edge, kron_own, kron_side = [], [], [], []
    for b in range(3):
        radius = radii_ref[b]
        length, width = band_rows[b], band_cols[b]
        shape = (length, length)
        row_own.append(taper(radius, iota(shape, 0) - iota(shape, 1)).astype(BF16))
        shape = (2 * REACH, length)
        h, i = iota(shape, 0), iota(shape, 1)
        edge_weights = taper(radius, jnp.where(h < REACH, length + h - i, h - 2 * REACH - i))
        edges = []
        for s in shifts:
            head_ok = jnp.where(lat + 1 < n_lat, 1.0, 0.0) if s == 1 else 0.0
            tail_ok = jnp.where(lat > 0, 1.0, 0.0) if s == n_lat - 1 else 0.0
            edges.append((edge_weights * jnp.where(h < REACH, head_ok, tail_ok)).astype(BF16))
        row_edge.append(edges)

        tall = levels * width
        c_shift, l_mask = log2(width), levels - 1
        pick_level = one_hot((iota((tall, levels), 0) >> c_shift) == iota((tall, levels), 1))
        pick_col = one_hot((iota((tall, width), 0) & (width - 1)) == iota((tall, width), 1))
        by_level = dot(pick_level, vertical_ref[b]).astype(BF16)

        def kron(weights, source_level, source_place):
            left = dot(by_level, source_level)
            right = dot(dot(pick_col, weights.astype(BF16)).astype(BF16), source_place)
            return (left * right).astype(BF16)

        shape = (width, width)
        own_weights = taper(radius, iota(shape, 1) - iota(shape, 0))
        level_of = one_hot(iota((levels, tall), 0) == (iota((levels, tall), 1) >> c_shift))
        place_of = one_hot(iota((width, tall), 0) == (iota((width, tall), 1) & (width - 1)))
        kron_own.append(kron(own_weights, level_of, place_of))
        shape = (width, 2 * REACH)
        c, q = iota(shape, 0), iota(shape, 1)
        side_weights = taper(radius, jnp.where(q < REACH, q - REACH - c, width + q - REACH - c))
        wide = 2 * levels * REACH
        r_shift = log2(REACH)
        level_of = one_hot(
            iota((levels, wide), 0) == ((iota((levels, wide), 1) >> r_shift) & l_mask)
        )
        spot = iota((2 * REACH, wide), 1)
        spot = ((spot >> log2(levels * REACH)) << r_shift) + (spot & (REACH - 1))
        place_of = one_hot(iota((2 * REACH, wide), 0) == spot)
        kron_side.append(kron(side_weights, level_of, place_of))

    loads[3].wait()
    member_cells = flat(members_ref[...])
    group = max(1, min(levels, 256 // cols))
    restricted = [None]
    for b in (1, 2):
        factor = FACTORS[b]
        picks_ref = mid_picks_ref if b == 1 else coarse_picks_ref
        length, width = band_rows[b], band_cols[b]
        row_pick = pick_vector(picks_ref, lat * length, length, length)
        target = (iota((length, rows), 0) * factor).astype(F32) + row_pick
        by_rows = dot_nt(member_cells, one_hot(iota((length, rows), 1).astype(F32) == target)).astype(BF16)
        tall = group * width
        col_pick = pick_vector(picks_ref, n_lat * length + lon * width, tall, width)
        target = (iota((tall, group * cols), 0) * factor).astype(F32) + col_pick
        chooser = one_hot(iota((tall, group * cols), 1).astype(F32) == target)
        pieces = []
        for m in range(count):
            parts = []
            for g in range(levels // group):
                first = (m * levels + g * group) * cols
                parts.append(dot(chooser, by_rows[first : first + group * cols]))
            pieces.append(jnp.concatenate(parts, axis=0))
        restricted.append(pieces)

    own_filtered = [dot(flat(owns[b][...]), row_own[b]) for b in range(3)]
    for copy in lat_copies:
        copy.wait_recv()
    local = []
    for b in range(3):
        tall = levels * band_cols[b]
        across = own_filtered[b]
        for k in range(len(shifts)):
            strip = strip_in[k, :, starts[b] : starts[b] + count * tall]
            across = across + dot_tn(strip, row_edge[b][k])
        across = across.astype(BF16)
        local.append([dot(kron_own[b], across[m * tall : (m + 1) * tall]) for m in range(count)])

    for copy in lon_copies:
        copy.wait_recv()
    wide = 2 * levels * REACH
    sums = []
    for b in range(3):
        halo = dot(flat(sides[b][...]), row_own[b])
        total = None
        for m in range(count):
            across = halo[m * wide : (m + 1) * wide]
            for k in range(len(shifts)):
                corner = jnp.concatenate(
                    [corner_in[k, b * count + m, 0], corner_in[k, b * count + m, 1]], axis=1
                )
                across = across + dot_tn(corner, row_edge[b][k])
            filtered = local[b][m] + dot(kron_side[b], across.astype(BF16))
            if b == 0:
                member = flat(members_ref[m]).astype(F32)
            else:
                member = restricted[b][m]
            product = member * filtered
            total = product if total is None else total + product
        sums.append(total)

    field = [sums[0][g * group * cols : (g + 1) * group * cols] for g in range(levels // group)]
    for b in (1, 2):
        f_shift = log2(FACTORS[b])
        length, width = band_rows[b], band_cols[b]
        repeat = one_hot(iota((length, rows), 0) == (iota((length, rows), 1) >> f_shift))
        spread = dot(sums[b].astype(BF16), repeat).astype(BF16)
        tall = group * width
        shape = (group * cols, tall)
        repeat = one_hot((iota(shape, 0) >> f_shift) == iota(shape, 1))
        for g in range(levels // group):
            field[g] = field[g] + dot(repeat, spread[g * tall : (g + 1) * tall])
    whole = jnp.concatenate(field, axis=0)
    block = levels * cols // n_mem
    field_ref[...] = whole.reshape(n_mem, block, rows)
    sum_out[...] = whole.reshape(n_mem, block, rows).astype(BF16)

    sum_copies = []
    for s in range(1, n_mem):
        there = lax.rem(mem + s, n_mem)
        sum_copies.append(
            remote(
                sum_out.at[there],
                sum_in.at[s - 1],
                sum_send.at[s - 1],
                sum_recv.at[s - 1],
                {"mem": there},
            )
        )
    for copy in sum_copies:
        copy.start()
    total = field_ref[mem]
    for s, copy in enumerate(sum_copies):
        copy.wait_recv()
        total = total + sum_in[s].astype(F32)
    out_ref[...] = total
    for copy in lon_copies + lat_copies + sum_copies:
        copy.wait_send()


def on_device(
    members,
    control_fine,
    control_mid,
    control_coarse,
    vertical,
    mid_picks,
    coarse_picks,
    band_radii,
):
    n_mem, n_lat, n_lon = (lax.axis_size(axis) for axis in ("mem", "lat", "lon"))
    shifts = sorted({1, n_lat - 1}) if n_lat > 1 else []
    slots = max(1, len(shifts))
    count, levels, cols, rows = members.shape
    controls = (control_fine, control_mid, control_coarse)
    block = levels * cols // n_mem
    strip_lanes = sum(count * levels * c.shape[2] for c in controls)
    corner_lanes = levels * REACH
    any_spec = pl.BlockSpec(memory_space=pl.ANY)
    vmem_spec = pl.BlockSpec(memory_space=pltpu.VMEM)
    dma = pltpu.SemaphoreType.DMA
    scratch = (
        [pltpu.VMEM(members.shape, BF16)]
        + [pltpu.VMEM(c.shape, BF16) for c in controls]
        + [pltpu.VMEM((count, 2, levels, REACH, c.shape[3]), BF16) for c in controls]
        + [
            pltpu.VMEM((2 * REACH, strip_lanes), BF16),
            pltpu.VMEM((slots, 2 * REACH, strip_lanes), BF16),
            pltpu.VMEM((2, 3 * count, 2 * REACH, corner_lanes), BF16),
            pltpu.VMEM((slots, 3 * count, 2, 2 * REACH, corner_lanes), BF16),
            pltpu.VMEM((n_mem, block, rows), F32),
            pltpu.VMEM((n_mem, block, rows), BF16),
            pltpu.VMEM((n_mem, block, rows), BF16),
            dma((4,)),
            dma((6,)),
            dma((6,)),
            dma((slots,)),
            dma((slots,)),
            dma((2 * slots,)),
            dma((2 * slots,)),
            dma((n_mem,)),
            dma((n_mem,)),
        ]
    )
    summed = pl.pallas_call(
        functools.partial(kernel, (n_mem, n_lat, n_lon, shifts)),
        out_shape=jax.ShapeDtypeStruct((block, rows), F32),
        in_specs=[any_spec] * 4 + [vmem_spec] * 3 + [pl.BlockSpec(memory_space=pltpu.SMEM)],
        out_specs=vmem_spec,
        scratch_shapes=scratch,
        compiler_params=pltpu.CompilerParams(
            collective_id=0, has_side_effects=True, vmem_limit_bytes=48 << 20
        ),
    )(
        *((members,) + controls),
        vertical,
        mid_picks[None, :],
        coarse_picks[None, :],
        band_radii,
    )
    scale = 1.0 / math.sqrt(count * n_mem - 1)
    return (summed * scale)[None, :, :]


def solution(mesh):
    placed = (
        P("mem", None, "lon", "lat"),
        P("mem", None, "lon", "lat"),
        P("mem", None, "lon", "lat"),
        P("mem", None, "lon", "lat"),
        P(),
        P(),
        P(),
        P(),
    )
    return jax.shard_map(
        on_device, mesh=mesh, in_specs=placed, out_specs=P("lon", "mem", "lat"), check_vma=False
    )
```

time: 159 us -> 29.4 us (0.18)
  matrix products: 70.2 us -> 0 us
  waiting for transfers between devices: 28.9 us -> 0 us
  Pallas kernels: 0 us -> 23.1 us
  blocking collectives: 16 us -> 0 us
  between operations: 15.3 us -> 0.02 us
  starting transfers between devices: 14 us -> 0 us
  other arithmetic: 7.71 us -> 0.67 us
    dot_general x11 -> x0, matrix products: 70.2 us -> none  [the longest x2 23.1 us: rim_filter(): jnp.einsum('cj,mkjr->mkcr', col_matrix, wrapped, preferred_element_type=j...]
    reduce_scatter x3 -> x0, waiting for transfers between devices: 28.8 us -> none  [on_device(): reduced = lax.psum_scatter(flat, 'mem', scatter_dimension=0, tiled=True)]
    pallas_call x0 -> x1, Pallas kernels: none -> 23.1 us  [on_device(): pl.pallas_call(functools.partial(kernel, (n_mem, n_lat, n_lon, shifts)),...]
    all_gather x2 -> x0, blocking collectives: 16 us -> none  [the longest x1 9.94 us: whole_filter(): gathered = lax.all_gather(mixed, 'lat', axis=3, tiled=True)]
    ppermute x8 -> x0, starting transfers between devices: 13.9 us -> none  [the longest x4 9.31 us: extended(): lax.ppermute(tail, axis, [(i, (i + 1) % count) for i in range(ends)])]
    unnamed x12 -> x14, local copies, waits for them, and re-layouts: 0.03 us -> 4.54 us
    slice x9 -> x0, local copies, waits for them, and re-layouts: 3.06 us -> none  [the longest x3 2.16 us: band_matrix(): weight_wide[tap_index]]
    convert_element_type x3 -> x0, other arithmetic: 1.87 us -> none  [band_matrix(): weight_wide = weights.astype(jnp.float32)]
  transfers between devices with their start and end apart: 11 -> 0, of which waited for: 2 -> 0; matrix products, arithmetic and copies ran while one was open for 34% -> 0% of each run, Pallas kernels for 0% -> 0%
where the time goes in v1:
time: 29.4 us; the launch traced here: 29 us
  Pallas kernels  23.1 us (79%)
  local copies, waits for them, and re-layouts  5.25 us (18%)
  other arithmetic  0.67 us (2%)
    pallas_call x1, Pallas kernels, on_device(): pl.pallas_call(functools.partial(kernel, (n_mem, n_lat, n_lon, shifts)),...  23.1 us
    unnamed x14, local copies, waits for them, and re-layouts  4.54 us
    broadcast_in_dim x1, local copies, waits for them, and re-layouts, on_device(): mid_picks[None, :]  0.71 us
    broadcast_in_dim x1, other arithmetic, on_device(): return (summed * scale)[None, :, :]  0.67 us

profile of v1, /device:TPU:0, one launch (start us, length us, event | category | flops | bytes accessed | tf_op | source)
XLA Modules:
  0.0 29.0 jit_solution(18041434598683566483)
XLA Ops:
  0.0 0.0 copy-start.5
  0.0 0.0 copy-start.6
  0.0 0.7 %broadcast_in_dim.9.mid_picks_ref = s32[1,320]{1,0:T(1,128)S(1)} reshape(s32[320]{0:T(512)} %param.13) | data formatting | bytes 2560 | tf_op jit(solution)/shard_map/broadcast_in_dim | solution.py:411
  0.7 0.0 copy-done.5
  0.7 0.0 copy-done.6
  0.7 0.0 copy-start
  0.7 1.0 %copy-done = bf16[2,16,32,256]{3,2,1,0:T(8,128)(2,1)S(1)} copy-done((bf16[2,16,32,256]{3,2,1,0:T(8,128)(2,1)S(1)}, bf16[2,16,32,256]{3,2,1,0:T(8,128)(2,1)}, u32[]{:S(2)}) %copy-start) | copy-done | bytes 524312
  1.8 0.0 copy-start.1
  1.8 1.0 %copy-done.1 = bf16[2,16,32,256]{3,2,1,0:T(8,128)(2,1)S(1)} copy-done((bf16[2,16,32,256]{3,2,1,0:T(8,128)(2,1)S(1)}, bf16[2,16,32,256]{3,2,1,0:T(8,128)(2,1)}, u32[]{:S(2)}) %copy-start.1) | copy-done | bytes 524312
  2.8 0.0 copy-start.2
  2.8 0.9 %copy-done.2 = bf16[2,16,16,128]{3,2,1,0:T(8,128)(2,1)S(1)} copy-done((bf16[2,16,16,128]{3,2,1,0:T(8,128)(2,1)S(1)}, bf16[2,16,16,128]{3,2,1,0:T(8,128)(2,1)}, u32[]{:S(2)}) %copy-start.2) | copy-done | bytes 131096
  3.7 0.0 copy-start.3
  3.7 0.8 %copy-done.3 = bf16[2,16,8,64]{3,2,1,0:T(8,128)(2,1)S(1)} copy-done((bf16[2,16,8,64]{3,2,1,0:T(8,128)(2,1)S(1)}, bf16[2,16,8,64]{3,2,1,0:T(8,128)(2,1)}, u32[]{:S(2)}) %copy-start.3) | copy-done | bytes 32792
  4.6 0.0 copy-start.4
  4.6 0.7 %copy-done.4 = bf16[3,16,16]{2,1,0:T(8,128)(2,1)S(1)} copy-done((bf16[3,16,16]{2,1,0:T(8,128)(2,1)S(1)}, bf16[3,16,16]{2,1,0:T(8,128)(2,1)}, u32[]{:S(2)}) %copy-start.4) | copy-done | bytes 1560
  5.3 23.1 %shard_map.82 = f32[128,256]{1,0:T(8,128)S(1)} custom-call(bf16[2,16,32,256]{3,2,1,0:T(8,128)(2,1)S(1)} %copy-done, bf16[2,16,32,256]{3,2,1,0:T(8,128)(2,1)S(1)} %copy-done.1, bf16[2,16,16,128]{3,2,1,0:T(8,128)(2,1)S(1)} %copy-done.2, bf16[2,16,8,64]{3,2,1,0:T(8,128)(2,1)S(1)} %copy-done.3, bf16[3,16,16]{2,1,0:T(8,128)(2,1)S(1)} %copy-done.4, ...), custom_call_target="tpu_custom_call" | custom-call | tf_op jit(solution)/shard_map/pallas_call | solution.py:399
  28.3 0.7 %multiply_bitcast_fusion = f32[1,128,256]{2,1,0:T(8,128)} fusion(f32[128,256]{1,0:T(8,128)S(1)} %shard_map.82), kind=kLoop, calls=%fused_computation | loop fusion | flops 32768 | bytes 262144 | tf_op jit(solution)/shard_map/broadcast_in_dim | solution.py:416
Async XLA Ops:
  0.0 0.7 %copy-start.5 = (s32[160]{0:T(256)S(1)}, s32[160]{0:T(256)}, u32[]{:S(2)}) copy-start(s32[160]{0:T(256)} %param.14) | copy-start | bytes 1924
  0.0 0.7 %copy-start.6 = (s32[3]{0:T(128)S(1)}, s32[3]{0:T(128)}, u32[]{:S(2)}) copy-start(s32[3]{0:T(128)} %radii_ref.1) | copy-start | bytes 40
  0.7 1.0 %copy-start = (bf16[2,16,32,256]{3,2,1,0:T(8,128)(2,1)S(1)}, bf16[2,16,32,256]{3,2,1,0:T(8,128)(2,1)}, u32[]{:S(2)}) copy-start(bf16[2,16,32,256]{3,2,1,0:T(8,128)(2,1)} %members_hbm.1) | copy-start | bytes 1572868
  1.8 1.0 %copy-start.1 = (bf16[2,16,32,256]{3,2,1,0:T(8,128)(2,1)S(1)}, bf16[2,16,32,256]{3,2,1,0:T(8,128)(2,1)}, u32[]{:S(2)}) copy-start(bf16[2,16,32,256]{3,2,1,0:T(8,128)(2,1)} %fine_hbm.1) | copy-start | bytes 1572868
  2.8 0.9 %copy-start.2 = (bf16[2,16,16,128]{3,2,1,0:T(8,128)(2,1)S(1)}, bf16[2,16,16,128]{3,2,1,0:T(8,128)(2,1)}, u32[]{:S(2)}) copy-start(bf16[2,16,16,128]{3,2,1,0:T(8,128)(2,1)} %mid_hbm.1) | copy-start | bytes 393220
  3.7 0.8 %copy-start.3 = (bf16[2,16,8,64]{3,2,1,0:T(8,128)(2,1)S(1)}, bf16[2,16,8,64]{3,2,1,0:T(8,128)(2,1)}, u32[]{:S(2)}) copy-start(bf16[2,16,8,64]{3,2,1,0:T(8,128)(2,1)} %coarse_hbm.1) | copy-start | bytes 98308
  4.6 0.7 %copy-start.4 = (bf16[3,16,16]{2,1,0:T(8,128)(2,1)S(1)}, bf16[3,16,16]{2,1,0:T(8,128)(2,1)}, u32[]{:S(2)}) copy-start(bf16[3,16,16]{2,1,0:T(8,128)(2,1)} %vertical_ref.1) | copy-start | bytes 4612

commit v2 on v1

--- a/solution.py
+++ b/solution.py
@@ -79,11 +79,15 @@
     fine_hbm,
     mid_hbm,
     coarse_hbm,
+    vertical_hbm,
+    mid_picks_hbm,
+    coarse_picks_hbm,
+    radii_hbm,
+    out_ref,
     vertical_ref,
     mid_picks_ref,
     coarse_picks_ref,
     radii_ref,
-    out_ref,
     members_ref,
     own0,
     own1,
@@ -122,7 +126,18 @@
         pltpu.make_async_copy(src, dst, load_sem.at[i])
         for i, (src, dst) in enumerate(zip(controls_hbm + (members_hbm,), owns + (members_ref,)))
     ]
-    for load in loads:
+    tables = [
+        pltpu.make_async_copy(src, dst, load_sem.at[4 + i])
+        for i, (src, dst) in enumerate(
+            (
+                (radii_hbm, radii_ref),
+                (vertical_hbm, vertical_ref),
+                (mid_picks_hbm, mid_picks_ref.at[0]),
+                (coarse_picks_hbm, coarse_picks_ref.at[0]),
+            )
+        )
+    ]
+    for load in tables + loads:
         load.start()
 
     partners = [{"lon": before}, {"lon": after}]
@@ -208,6 +223,8 @@
     for copy in lat_copies:
         copy.start()
 
+    for load in tables:
+        load.wait()
     row_own, row_edge, kron_own, kron_side = [], [], [], []
     for b in range(3):
         radius = radii_ref[b]
@@ -370,11 +387,17 @@
     block = levels * cols // n_mem
     strip_lanes = sum(count * levels * c.shape[2] for c in controls)
     corner_lanes = levels * REACH
-    any_spec = pl.BlockSpec(memory_space=pl.ANY)
+    hbm_spec = pl.BlockSpec(memory_space=pltpu.HBM)
     vmem_spec = pl.BlockSpec(memory_space=pltpu.VMEM)
     dma = pltpu.SemaphoreType.DMA
     scratch = (
-        [pltpu.VMEM(members.shape, BF16)]
+        [
+            pltpu.VMEM(vertical.shape, BF16),
+            pltpu.VMEM((1,) + mid_picks.shape, jnp.int32),
+            pltpu.VMEM((1,) + coarse_picks.shape, jnp.int32),
+            pltpu.SMEM(band_radii.shape, jnp.int32),
+            pltpu.VMEM(members.shape, BF16),
+        ]
         + [pltpu.VMEM(c.shape, BF16) for c in controls]
         + [pltpu.VMEM((count, 2, levels, REACH, c.shape[3]), BF16) for c in controls]
         + [
@@ -385,7 +408,7 @@
             pltpu.VMEM((n_mem, block, rows), F32),
             pltpu.VMEM((n_mem, block, rows), BF16),
             pltpu.VMEM((n_mem, block, rows), BF16),
-            dma((4,)),
+            dma((8,)),
             dma((6,)),
             dma((6,)),
             dma((slots,)),
@@ -399,17 +422,17 @@
     summed = pl.pallas_call(
         functools.partial(kernel, (n_mem, n_lat, n_lon, shifts)),
         out_shape=jax.ShapeDtypeStruct((block, rows), F32),
-        in_specs=[any_spec] * 4 + [vmem_spec] * 3 + [pl.BlockSpec(memory_space=pltpu.SMEM)],
+        in_specs=[hbm_spec] * 8,
         out_specs=vmem_spec,
         scratch_shapes=scratch,
         compiler_params=pltpu.CompilerParams(
-            collective_id=0, has_side_effects=True, vmem_limit_bytes=48 << 20
+            collective_id=0, has_side_effects=True, vmem_limit_bytes=67043328
         ),
     )(
         *((members,) + controls),
         vertical,
-        mid_picks[None, :],
-        coarse_picks[None, :],
+        mid_picks,
+        coarse_picks,
         band_radii,
     )
     scale = 1.0 / math.sqrt(count * n_mem - 1)

time: 29.4 us -> 24.8 us (0.84)
  local copies, waits for them, and re-layouts: 5.25 us -> 0 us
  other arithmetic: 0.67 us -> 1.57 us
    unnamed x14 -> x0, local copies, waits for them, and re-layouts: 4.54 us -> none
    broadcast_in_dim x1, other arithmetic: 0.67 us -> 1.57 us  [on_device(): return (summed * scale)[None, :, :]]
    broadcast_in_dim x1 -> x0, local copies, waits for them, and re-layouts: 0.71 us -> none  [on_device(): mid_picks[None, :]]
where the time goes in v2:
time: 24.8 us; the launch traced here: 24.6 us
  Pallas kernels  23.1 us (93%)
  other arithmetic  1.57 us (6%)
    pallas_call x1, Pallas kernels, on_device(): pl.pallas_call(functools.partial(kernel, (n_mem, n_lat, n_lon, shifts)),...  23.1 us
    broadcast_in_dim x1, other arithmetic, on_device(): return (summed * scale)[None, :, :]  1.57 us

profile of v2, /device:TPU:0, one launch (start us, length us, event | category | flops | bytes accessed | tf_op | source)
XLA Modules:
  0.0 24.6 jit_solution(5948830164831324037)
XLA Ops:
  0.0 23.1 %shard_map.82 = f32[128,256]{1,0:T(8,128)} custom-call(bf16[2,16,32,256]{3,2,1,0:T(8,128)(2,1)} %members_hbm.1, bf16[2,16,32,256]{3,2,1,0:T(8,128)(2,1)} %fine_hbm.1, bf16[2,16,16,128]{3,2,1,0:T(8,128)(2,1)} %mid_hbm.1, bf16[2,16,8,64]{3,2,1,0:T(8,128)(2,1)} %coarse_hbm.1, bf16[3,16,16]{2,1,0:T(8,128)(2,1)} %vertical_hbm.1, s32[320]{0:T(512)} %mid_picks_hbm.1, ...), custom_call_target="tpu_custom_call" | custom-call | tf_op jit(solution)/shard_map/pallas_call | solution.py:422
  23.1 1.6 %multiply_bitcast_fusion = f32[1,128,256]{2,1,0:T(8,128)} fusion(f32[128,256]{1,0:T(8,128)} %shard_map.82), kind=kLoop, calls=%fused_computation | loop fusion | flops 32768 | bytes 262144 | tf_op jit(solution)/shard_map/broadcast_in_dim | solution.py:439

commit v3 on v2

--- a/solution.py
+++ b/solution.py
@@ -99,20 +99,15 @@
     strip_in,
     corner_out,
     corner_in,
-    field_ref,
-    sum_out,
-    sum_in,
-    load_sem,
-    lon_send,
-    lon_recv,
-    strip_send,
-    strip_recv,
-    corner_send,
-    corner_recv,
-    sum_send,
-    sum_recv,
+    *rest,
+
 ):
-    n_mem, n_lat, n_lon, shifts = sizes
+    n_mem, n_lat, n_lon, shifts, parts = sizes
+    field_refs, sum_outs, sum_ins = (
+        rest[i * len(parts) : (i + 1) * len(parts)] for i in range(3)
+    )
+    load_sem, lon_send, lon_recv, strip_send, strip_recv = rest[3 * len(parts) :][:5]
+    corner_send, corner_recv, sum_send, sum_recv = rest[3 * len(parts) :][5:]
     mem, lat, lon = lax.axis_index("mem"), lax.axis_index("lat"), lax.axis_index("lon")
     count, levels, cols, rows = members_ref.shape
     controls_hbm = (fine_hbm, mid_hbm, coarse_hbm)
@@ -156,6 +151,28 @@
             src_ref=src, dst_ref=dst, send_sem=send, recv_sem=recv, device_id=device, device_id_type=MESH
         )
 
+    def sum_copy(p, s):
+        there = lax.rem(mem + s, n_mem)
+        return remote(
+            sum_outs[p].at[there],
+            sum_ins[p].at[s - 1],
+            sum_send.at[p, s - 1],
+            sum_recv.at[p, s - 1],
+            {"mem": there},
+        )
+
+    def start_sum(p, dest):
+        @pl.when(mem != dest)
+        def _():
+            slot = lax.rem(dest - mem + n_mem, n_mem) - 1
+            remote(
+                sum_outs[p].at[dest],
+                sum_ins[p].at[slot],
+                sum_send.at[p, slot],
+                sum_recv.at[p, slot],
+                {"mem": dest},
+            ).start()
+
     lon_copies = []
     for b in range(3):
         width = band_cols[b]
@@ -177,7 +194,7 @@
                 {"lon": before},
             )
         )
-    for copy in lon_copies:
+    for copy in lon_copies[4:] + lon_copies[2:4] + lon_copies[:2]:
         copy.start()
 
     starts = []
@@ -241,34 +258,46 @@
             edges.append((edge_weights * jnp.where(h < REACH, head_ok, tail_ok)).astype(BF16))
         row_edge.append(edges)
 
+        by_parts_own, by_parts_side = [], []
         tall = levels * width
-        c_shift, l_mask = log2(width), levels - 1
-        pick_level = one_hot((iota((tall, levels), 0) >> c_shift) == iota((tall, levels), 1))
-        pick_col = one_hot((iota((tall, width), 0) & (width - 1)) == iota((tall, width), 1))
-        by_level = dot(pick_level, vertical_ref[b]).astype(BF16)
-
-        def kron(weights, source_level, source_place):
-            left = dot(by_level, source_level)
-            right = dot(dot(pick_col, weights.astype(BF16)).astype(BF16), source_place)
-            return (left * right).astype(BF16)
-
+        level_of = one_hot(iota((levels, tall), 0) == (iota((levels, tall), 1) >> log2(width)))
+        place_of = one_hot(iota((width, tall), 0) == (iota((width, tall), 1) & (width - 1)))
+        wide = 2 * levels * REACH
+        r_shift = log2(REACH)
+        side_level_of = one_hot(
+            iota((levels, wide), 0) == ((iota((levels, wide), 1) >> r_shift) & (levels - 1))
+        )
+        spot = iota((2 * REACH, wide), 1)
+        spot = ((spot >> log2(levels * REACH)) << r_shift) + (spot & (REACH - 1))
+        side_place_of = one_hot(iota((2 * REACH, wide), 0) == spot)
         shape = (width, width)
-        own_weights = taper(radius, iota(shape, 1) - iota(shape, 0))
-        level_of = one_hot(iota((levels, tall), 0) == (iota((levels, tall), 1) >> c_shift))
-        place_of = one_hot(iota((width, tall), 0) == (iota((width, tall), 1) & (width - 1)))
-        kron_own.append(kron(own_weights, level_of, place_of))
+        own_weights = taper(radius, iota(shape, 1) - iota(shape, 0)).astype(BF16)
         shape = (width, 2 * REACH)
         c, q = iota(shape, 0), iota(shape, 1)
-        side_weights = taper(radius, jnp.where(q < REACH, q - REACH - c, width + q - REACH - c))
-        wide = 2 * levels * REACH
-        r_shift = log2(REACH)
-        level_of = one_hot(
-            iota((levels, wide), 0) == ((iota((levels, wide), 1) >> r_shift) & l_mask)
-        )
-        spot = iota((2 * REACH, wide), 1)
-        spot = ((spot >> log2(levels * REACH)) << r_shift) + (spot & (REACH - 1))
-        place_of = one_hot(iota((2 * REACH, wide), 0) == spot)
-        kron_side.append(kron(side_weights, level_of, place_of))
+        side_weights = jnp.where(q < REACH, q - REACH - c, width + q - REACH - c)
+        side_weights = taper(radius, side_weights).astype(BF16)
+        for part in parts if b == 0 else ("all",):
+            part_width = width_of(part, width)
+            tall = levels * part_width
+            pick_level = one_hot(
+                (iota((tall, levels), 0) >> log2(part_width)) == iota((tall, levels), 1)
+            )
+            column = column_of(part, iota((tall, width), 0) & (part_width - 1), width)
+            pick_col = one_hot(column == iota((tall, width), 1))
+            by_level = dot(pick_level, vertical_ref[b]).astype(BF16)
+
+            def kron(weights, source_level, source_place):
+                left = dot(by_level, source_level)
+                right = dot(dot(pick_col, weights).astype(BF16), source_place)
+                return (left * right).astype(BF16)
+
+            by_parts_own.append(kron(own_weights, level_of, place_of))
+            if part != "inner":
+                by_parts_side.append(kron(side_weights, side_level_of, side_place_of))
+            else:
+                by_parts_side.append(None)
+        kron_own.append(by_parts_own)
+        kron_side.append(by_parts_side)
 
     loads[3].wait()
     member_cells = flat(members_ref[...])
@@ -287,11 +316,11 @@
         chooser = one_hot(iota((tall, group * cols), 1).astype(F32) == target)
         pieces = []
         for m in range(count):
-            parts = []
+            picked = []
             for g in range(levels // group):
                 first = (m * levels + g * group) * cols
-                parts.append(dot(chooser, by_rows[first : first + group * cols]))
-            pieces.append(jnp.concatenate(parts, axis=0))
+                picked.append(dot(chooser, by_rows[first : first + group * cols]))
+            pieces.append(jnp.concatenate(picked, axis=0))
         restricted.append(pieces)
 
     own_filtered = [dot(flat(owns[b][...]), row_own[b]) for b in range(3)]
@@ -305,15 +334,20 @@
             strip = strip_in[k, :, starts[b] : starts[b] + count * tall]
             across = across + dot_tn(strip, row_edge[b][k])
         across = across.astype(BF16)
-        local.append([dot(kron_own[b], across[m * tall : (m + 1) * tall]) for m in range(count)])
-
-    for copy in lon_copies:
-        copy.wait_recv()
+        local.append(
+            [
+                [dot(part, across[m * tall : (m + 1) * tall]) for m in range(count)]
+                for part in kron_own[b]
+            ]
+        )
+
     wide = 2 * levels * REACH
-    sums = []
-    for b in range(3):
+
+    def side_cells(b):
+        for copy in lon_copies[2 * b : 2 * b + 2]:
+            copy.wait_recv()
         halo = dot(flat(sides[b][...]), row_own[b])
-        total = None
+        cells = []
         for m in range(count):
             across = halo[m * wide : (m + 1) * wide]
             for k in range(len(shifts)):
@@ -321,52 +355,100 @@
                     [corner_in[k, b * count + m, 0], corner_in[k, b * count + m, 1]], axis=1
                 )
                 across = across + dot_tn(corner, row_edge[b][k])
-            filtered = local[b][m] + dot(kron_side[b], across.astype(BF16))
-            if b == 0:
-                member = flat(members_ref[m]).astype(F32)
-            else:
-                member = restricted[b][m]
-            product = member * filtered
+            cells.append(across.astype(BF16))
+        return cells
+
+    spread = [None]
+    for b in (1, 2):
+        cells = side_cells(b)
+        total = None
+        for m in range(count):
+            product = restricted[b][m] * (local[b][0][m] + dot(kron_side[b][0], cells[m]))
             total = product if total is None else total + product
-        sums.append(total)
-
-    field = [sums[0][g * group * cols : (g + 1) * group * cols] for g in range(levels // group)]
-    for b in (1, 2):
-        f_shift = log2(FACTORS[b])
-        length, width = band_rows[b], band_cols[b]
-        repeat = one_hot(iota((length, rows), 0) == (iota((length, rows), 1) >> f_shift))
-        spread = dot(sums[b].astype(BF16), repeat).astype(BF16)
-        tall = group * width
-        shape = (group * cols, tall)
-        repeat = one_hot((iota(shape, 0) >> f_shift) == iota(shape, 1))
+        length = band_rows[b]
+        repeat = one_hot(iota((length, rows), 0) == (iota((length, rows), 1) >> log2(FACTORS[b])))
+        spread.append(dot(total.astype(BF16), repeat).astype(BF16))
+
+    block = levels * cols // n_mem
+    sum_copies = []
+    for p, part in enumerate(parts):
+        part_width = width_of(part, cols)
+        part_block = block * part_width // cols
+        cells = None if part == "inner" else side_cells(0)
+        fine = []
+        for m in range(count):
+            member = columns_of(part, members_ref[m].astype(F32))
+            filtered = local[0][p][m]
+            if cells is not None:
+                filtered = filtered + dot(kron_side[0][p], cells[m])
+            fine.append(member * filtered)
+        total = fine[0]
+        for product in fine[1:]:
+            total = total + product
+        tall = group * part_width
+        dests = n_mem * group // levels
         for g in range(levels // group):
-            field[g] = field[g] + dot(repeat, spread[g * tall : (g + 1) * tall])
-    whole = jnp.concatenate(field, axis=0)
-    block = levels * cols // n_mem
-    field_ref[...] = whole.reshape(n_mem, block, rows)
-    sum_out[...] = whole.reshape(n_mem, block, rows).astype(BF16)
-
-    sum_copies = []
-    for s in range(1, n_mem):
-        there = lax.rem(mem + s, n_mem)
-        sum_copies.append(
-            remote(
-                sum_out.at[there],
-                sum_in.at[s - 1],
-                sum_send.at[s - 1],
-                sum_recv.at[s - 1],
-                {"mem": there},
-            )
-        )
-    for copy in sum_copies:
-        copy.start()
-    total = field_ref[mem]
-    for s, copy in enumerate(sum_copies):
-        copy.wait_recv()
-        total = total + sum_in[s].astype(F32)
-    out_ref[...] = total
-    for copy in lon_copies + lat_copies + sum_copies:
+            piece = total[g * tall : (g + 1) * tall]
+            for b in (1, 2):
+                from_tall = group * band_cols[b]
+                r = iota((tall, from_tall), 0)
+                source = column_of(part, r & (part_width - 1), cols) >> log2(FACTORS[b])
+                source = ((r >> log2(part_width)) << log2(band_cols[b])) + source
+                repeat = one_hot(source == iota((tall, from_tall), 1))
+                piece = piece + dot(repeat, spread[b][g * from_tall : (g + 1) * from_tall])
+            piece = piece.reshape(-1, part_block, rows)
+            here = slice(g * piece.shape[0], (g + 1) * piece.shape[0])
+            field_refs[p][here] = piece
+            sum_outs[p][here] = piece.astype(BF16)
+            if levels // group == 1 or n_mem % (levels // group):
+                continue
+            for dest in range(g * dests, (g + 1) * dests):
+                start_sum(p, dest)
+        if levels // group == 1 or n_mem % (levels // group):
+            for dest in range(n_mem):
+                start_sum(p, dest)
+
+    for p, part in enumerate(parts):
+        total = field_refs[p][mem]
+        for s in range(1, n_mem):
+            sum_copy(p, s).wait_recv()
+            total = total + sum_ins[p][s - 1].astype(F32)
+        if part == "all":
+            out_ref[0] = total
+            continue
+        total = total.reshape(block // cols, -1, rows)
+        if part == "inner":
+            out_ref[:, REACH : cols - REACH, :] = total
+        else:
+            out_ref[:, :REACH, :] = total[:, :REACH, :]
+            out_ref[:, cols - REACH :, :] = total[:, REACH:, :]
+    for copy in lon_copies + lat_copies:
         copy.wait_send()
+    for p in range(len(parts)):
+        for s in range(1, n_mem):
+            sum_copy(p, s).wait_send()
+
+
+def width_of(part, width):
+    return {"inner": width - 2 * REACH, "outer": 2 * REACH, "all": width}[part]
+
+
+def column_of(part, place, width):
+    if part == "inner":
+        return place + REACH
+    if part == "outer":
+        return jnp.where(place < REACH, place, place + (width - 2 * REACH))
+    return place
+
+
+def columns_of(part, cells):
+    if part == "inner":
+        cells = cells[:, REACH : cells.shape[1] - REACH, :]
+    if part == "outer":
+        cells = jnp.concatenate(
+            [cells[:, :REACH, :], cells[:, cells.shape[1] - REACH :, :]], axis=1
+        )
+    return cells.reshape(-1, cells.shape[2])
 
 
 def on_device(
@@ -385,6 +467,10 @@
     count, levels, cols, rows = members.shape
     controls = (control_fine, control_mid, control_coarse)
     block = levels * cols // n_mem
+    inner = cols - 2 * REACH
+    split = block % cols == 0 and inner > 0 and inner & (inner - 1) == 0
+    parts = ("inner", "outer") if split else ("all",)
+    out_shape = (block // cols, cols, rows) if split else (1, block, rows)
     strip_lanes = sum(count * levels * c.shape[2] for c in controls)
     corner_lanes = levels * REACH
     hbm_spec = pl.BlockSpec(memory_space=pltpu.HBM)
@@ -405,9 +491,10 @@
             pltpu.VMEM((slots, 2 * REACH, strip_lanes), BF16),
             pltpu.VMEM((2, 3 * count, 2 * REACH, corner_lanes), BF16),
             pltpu.VMEM((slots, 3 * count, 2, 2 * REACH, corner_lanes), BF16),
-            pltpu.VMEM((n_mem, block, rows), F32),
-            pltpu.VMEM((n_mem, block, rows), BF16),
-            pltpu.VMEM((n_mem, block, rows), BF16),
+        ]
+        + [pltpu.VMEM((n_mem, block * width_of(p, cols) // cols, rows), F32) for p in parts]
+        + [pltpu.VMEM((n_mem, block * width_of(p, cols) // cols, rows), BF16) for p in parts] * 2
+        + [
             dma((8,)),
             dma((6,)),
             dma((6,)),
@@ -415,13 +502,13 @@
             dma((slots,)),
             dma((2 * slots,)),
             dma((2 * slots,)),
-            dma((n_mem,)),
-            dma((n_mem,)),
+            dma((len(parts), n_mem)),
+            dma((len(parts), n_mem)),
         ]
     )
     summed = pl.pallas_call(
-        functools.partial(kernel, (n_mem, n_lat, n_lon, shifts)),
-        out_shape=jax.ShapeDtypeStruct((block, rows), F32),
+        functools.partial(kernel, (n_mem, n_lat, n_lon, shifts, parts)),
+        out_shape=jax.ShapeDtypeStruct(out_shape, F32),
         in_specs=[hbm_spec] * 8,
         out_specs=vmem_spec,
         scratch_shapes=scratch,
@@ -436,7 +523,7 @@
         band_radii,
     )
     scale = 1.0 / math.sqrt(count * n_mem - 1)
-    return (summed * scale)[None, :, :]
+    return (summed * scale).reshape(1, block, rows)
 
 
 def solution(mesh):

time: 24.8 us -> 21.6 us (0.87)
  Pallas kernels: 23.1 us -> 19.8 us
    pallas_call x1, Pallas kernels: 23.1 us -> 19.8 us  [on_device(): pl.pallas_call(functools.partial(kernel, (n_mem, n_lat, n_lon, shifts, pa...]
    broadcast_in_dim x1 -> x0, other arithmetic: 1.57 us -> none  [on_device(): return (summed * scale)[None, :, :]]
    mul x0 -> x1, other arithmetic: none -> 1.57 us  [on_device(): return (summed * scale).reshape(1, block, rows)]
where the time goes in v3:
time: 21.6 us; the launch traced here: 21.4 us
  Pallas kernels  19.8 us (92%)
  other arithmetic  1.57 us (7%)
    pallas_call x1, Pallas kernels, on_device(): pl.pallas_call(functools.partial(kernel, (n_mem, n_lat, n_lon, shifts, pa...  19.8 us
    mul x1, other arithmetic, on_device(): return (summed * scale).reshape(1, block, rows)  1.57 us

profile of v3, /device:TPU:0, one launch (start us, length us, event | category | flops | bytes accessed | tf_op | source)
XLA Modules:
  0.0 21.4 jit_solution(17220600510409398666)
XLA Ops:
  0.0 19.8 %shard_map.82 = f32[4,32,256]{2,1,0:T(8,128)} custom-call(bf16[2,16,32,256]{3,2,1,0:T(8,128)(2,1)} %members_hbm.1, bf16[2,16,32,256]{3,2,1,0:T(8,128)(2,1)} %fine_hbm.1, bf16[2,16,16,128]{3,2,1,0:T(8,128)(2,1)} %mid_hbm.1, bf16[2,16,8,64]{3,2,1,0:T(8,128)(2,1)} %coarse_hbm.1, bf16[3,16,16]{2,1,0:T(8,128)(2,1)} %vertical_hbm.1, s32[320]{0:T(512)} %mid_picks_hbm.1, ...), custom_call_target="tpu_custom_call" | custom-call | tf_op jit(solution)/shard_map/pallas_call | solution.py:509
  19.8 1.6 %broadcast_multiply_fusion = f32[4,32,256]{2,1,0:T(8,128)} fusion(f32[4,32,256]{2,1,0:T(8,128)} %shard_map.82), kind=kLoop, calls=%fused_computation | loop fusion | flops 32768 | bytes 262144 | tf_op jit(solution)/shard_map/mul | solution.py:526

commit v4 on v3

--- a/solution.py
+++ b/solution.py
@@ -144,65 +144,13 @@
     barrier = pltpu.get_barrier_semaphore()
     for partner in partners:
         pl.semaphore_signal(barrier, inc=1, device_id=partner, device_id_type=MESH)
-    pl.semaphore_wait(barrier, len(partners))
-
-    def remote(src, dst, send, recv, device):
-        return pltpu.make_async_remote_copy(
-            src_ref=src, dst_ref=dst, send_sem=send, recv_sem=recv, device_id=device, device_id_type=MESH
-        )
-
-    def sum_copy(p, s):
-        there = lax.rem(mem + s, n_mem)
-        return remote(
-            sum_outs[p].at[there],
-            sum_ins[p].at[s - 1],
-            sum_send.at[p, s - 1],
-            sum_recv.at[p, s - 1],
-            {"mem": there},
-        )
-
-    def start_sum(p, dest):
-        @pl.when(mem != dest)
-        def _():
-            slot = lax.rem(dest - mem + n_mem, n_mem) - 1
-            remote(
-                sum_outs[p].at[dest],
-                sum_ins[p].at[slot],
-                sum_send.at[p, slot],
-                sum_recv.at[p, slot],
-                {"mem": dest},
-            ).start()
-
-    lon_copies = []
-    for b in range(3):
-        width = band_cols[b]
-        lon_copies.append(
-            remote(
-                controls_hbm[b].at[:, :, width - REACH : width, :],
-                sides[b].at[:, 0],
-                lon_send.at[2 * b],
-                lon_recv.at[2 * b],
-                {"lon": after},
-            )
-        )
-        lon_copies.append(
-            remote(
-                controls_hbm[b].at[:, :, 0:REACH, :],
-                sides[b].at[:, 1],
-                lon_send.at[2 * b + 1],
-                lon_recv.at[2 * b + 1],
-                {"lon": before},
-            )
-        )
-    for copy in lon_copies[4:] + lon_copies[2:4] + lon_copies[:2]:
-        copy.start()
 
     starts = []
     place = 0
     for b in range(3):
         starts.append(place)
         place += count * levels * band_cols[b]
-    lat_copies = []
+    strip_copies, corner_copies = [], []
     for b in range(3):
         loads[b].wait()
     for b in range(3):
@@ -220,29 +168,9 @@
             for m in range(count):
                 lanes = levels * REACH
                 corner_out[side, b * count + m] = packed[:, m * lanes : (m + 1) * lanes]
-    for k, s in enumerate(shifts):
-        slot = shifts.index((n_lat - s) % n_lat)
-        there = lax.rem(lat + s, n_lat)
-        lat_copies.append(
-            remote(strip_out, strip_in.at[slot], strip_send.at[slot], strip_recv.at[slot], {"lat": there})
-        )
-        for side in range(2):
-            target = before if side == 0 else after
-            lat_copies.append(
-                remote(
-                    corner_out.at[side],
-                    corner_in.at[slot, :, 1 - side],
-                    corner_send.at[2 * slot + side],
-                    corner_recv.at[2 * slot + side],
-                    {"lat": there, "lon": target},
-                )
-            )
-    for copy in lat_copies:
-        copy.start()
-
     for load in tables:
         load.wait()
-    row_own, row_edge, kron_own, kron_side = [], [], [], []
+    row_own, row_edge = [], []
     for b in range(3):
         radius = radii_ref[b]
         length, width = band_rows[b], band_cols[b]
@@ -258,7 +186,79 @@
             edges.append((edge_weights * jnp.where(h < REACH, head_ok, tail_ok)).astype(BF16))
         row_edge.append(edges)
 
-        by_parts_own, by_parts_side = [], []
+    pl.semaphore_wait(barrier, len(partners))
+
+    def remote(src, dst, send, recv, device):
+        return pltpu.make_async_remote_copy(
+            src_ref=src, dst_ref=dst, send_sem=send, recv_sem=recv, device_id=device, device_id_type=MESH
+        )
+
+    def sum_copy(p, s):
+        there = lax.rem(mem + s, n_mem)
+        return remote(
+            sum_outs[p].at[there],
+            sum_ins[p].at[s - 1],
+            sum_send.at[p, s - 1],
+            sum_recv.at[p, s - 1],
+            {"mem": there},
+        )
+
+    def start_sum(p, dest):
+        @pl.when(mem != dest)
+        def _():
+            slot = lax.rem(dest - mem + n_mem, n_mem) - 1
+            remote(
+                sum_outs[p].at[dest],
+                sum_ins[p].at[slot],
+                sum_send.at[p, slot],
+                sum_recv.at[p, slot],
+                {"mem": dest},
+            ).start()
+
+    lon_copies = []
+    for b in range(3):
+        width = band_cols[b]
+        lon_copies.append(
+            remote(
+                controls_hbm[b].at[:, :, width - REACH : width, :],
+                sides[b].at[:, 0],
+                lon_send.at[2 * b],
+                lon_recv.at[2 * b],
+                {"lon": after},
+            )
+        )
+        lon_copies.append(
+            remote(
+                controls_hbm[b].at[:, :, 0:REACH, :],
+                sides[b].at[:, 1],
+                lon_send.at[2 * b + 1],
+                lon_recv.at[2 * b + 1],
+                {"lon": before},
+            )
+        )
+
+    for k, s in enumerate(shifts):
+        slot = shifts.index((n_lat - s) % n_lat)
+        there = lax.rem(lat + s, n_lat)
+        strip_copies.append(
+            remote(strip_out, strip_in.at[slot], strip_send.at[slot], strip_recv.at[slot], {"lat": there})
+        )
+        for side in range(2):
+            target = before if side == 0 else after
+            corner_copies.append(
+                remote(
+                    corner_out.at[side],
+                    corner_in.at[slot, :, 1 - side],
+                    corner_send.at[2 * slot + side],
+                    corner_recv.at[2 * slot + side],
+                    {"lat": there, "lon": target},
+                )
+            )
+    for copy in corner_copies + strip_copies + lon_copies[4:] + lon_copies[2:4] + lon_copies[:2]:
+        copy.start()
+
+    def krons(b, part):
+        radius, width = radii_ref[b], band_cols[b]
         tall = levels * width
         level_of = one_hot(iota((levels, tall), 0) == (iota((levels, tall), 1) >> log2(width)))
         place_of = one_hot(iota((width, tall), 0) == (iota((width, tall), 1) & (width - 1)))
@@ -276,28 +276,24 @@
         c, q = iota(shape, 0), iota(shape, 1)
         side_weights = jnp.where(q < REACH, q - REACH - c, width + q - REACH - c)
         side_weights = taper(radius, side_weights).astype(BF16)
-        for part in parts if b == 0 else ("all",):
-            part_width = width_of(part, width)
-            tall = levels * part_width
-            pick_level = one_hot(
-                (iota((tall, levels), 0) >> log2(part_width)) == iota((tall, levels), 1)
-            )
-            column = column_of(part, iota((tall, width), 0) & (part_width - 1), width)
-            pick_col = one_hot(column == iota((tall, width), 1))
-            by_level = dot(pick_level, vertical_ref[b]).astype(BF16)
-
-            def kron(weights, source_level, source_place):
-                left = dot(by_level, source_level)
-                right = dot(dot(pick_col, weights).astype(BF16), source_place)
-                return (left * right).astype(BF16)
-
-            by_parts_own.append(kron(own_weights, level_of, place_of))
-            if part != "inner":
-                by_parts_side.append(kron(side_weights, side_level_of, side_place_of))
-            else:
-                by_parts_side.append(None)
-        kron_own.append(by_parts_own)
-        kron_side.append(by_parts_side)
+        part_width = width_of(part, width)
+        tall = levels * part_width
+        pick_level = one_hot((iota((tall, levels), 0) >> log2(part_width)) == iota((tall, levels), 1))
+        column = column_of(part, iota((tall, width), 0) & (part_width - 1), width)
+        pick_col = one_hot(column == iota((tall, width), 1))
+        by_level = dot(pick_level, vertical_ref[b]).astype(BF16)
+
+        def kron(weights, source_level, source_place):
+            left = dot(by_level, source_level)
+            right = dot(dot(pick_col, weights).astype(BF16), source_place)
+            return (left * right).astype(BF16)
+
+        own = kron(own_weights, level_of, place_of)
+        if part == "inner":
+            return own, None
+        return own, kron(side_weights, side_level_of, side_place_of)
+
+    kron = [krons(b, "all") if b else [krons(0, part) for part in parts] for b in range(3)]
 
     loads[3].wait()
     member_cells = flat(members_ref[...])
@@ -324,9 +320,9 @@
         restricted.append(pieces)
 
     own_filtered = [dot(flat(owns[b][...]), row_own[b]) for b in range(3)]
-    for copy in lat_copies:
+    for copy in strip_copies:
         copy.wait_recv()
-    local = []
+    across_own = []
     for b in range(3):
         tall = levels * band_cols[b]
         across = own_filtered[b]
@@ -334,12 +330,7 @@
             strip = strip_in[k, :, starts[b] : starts[b] + count * tall]
             across = across + dot_tn(strip, row_edge[b][k])
         across = across.astype(BF16)
-        local.append(
-            [
-                [dot(part, across[m * tall : (m + 1) * tall]) for m in range(count)]
-                for part in kron_own[b]
-            ]
-        )
+        across_own.append([across[m * tall : (m + 1) * tall] for m in range(count)])
 
     wide = 2 * levels * REACH
 
@@ -358,12 +349,15 @@
             cells.append(across.astype(BF16))
         return cells
 
+    for copy in corner_copies:
+        copy.wait_recv()
     spread = [None]
     for b in (1, 2):
         cells = side_cells(b)
         total = None
         for m in range(count):
-            product = restricted[b][m] * (local[b][0][m] + dot(kron_side[b][0], cells[m]))
+            filtered = dot(kron[b][0], across_own[b][m]) + dot(kron[b][1], cells[m])
+            product = restricted[b][m] * filtered
             total = product if total is None else total + product
         length = band_rows[b]
         repeat = one_hot(iota((length, rows), 0) == (iota((length, rows), 1) >> log2(FACTORS[b])))
@@ -374,13 +368,14 @@
     for p, part in enumerate(parts):
         part_width = width_of(part, cols)
         part_block = block * part_width // cols
+        kron_own, kron_side = kron[0][p]
         cells = None if part == "inner" else side_cells(0)
         fine = []
         for m in range(count):
             member = columns_of(part, members_ref[m].astype(F32))
-            filtered = local[0][p][m]
+            filtered = dot(kron_own, across_own[0][m])
             if cells is not None:
-                filtered = filtered + dot(kron_side[0][p], cells[m])
+                filtered = filtered + dot(kron_side, cells[m])
             fine.append(member * filtered)
         total = fine[0]
         for product in fine[1:]:
@@ -422,7 +417,7 @@
         else:
             out_ref[:, :REACH, :] = total[:, :REACH, :]
             out_ref[:, cols - REACH :, :] = total[:, REACH:, :]
-    for copy in lon_copies + lat_copies:
+    for copy in lon_copies + strip_copies + corner_copies:
         copy.wait_send()
     for p in range(len(parts)):
         for s in range(1, n_mem):

time: 21.6 us -> 21.5 us (level)
  no operation moved by 1% of the time
where the time goes in v4:
time: 21.5 us; the launch traced here: 21.3 us
  Pallas kernels  19.8 us (92%)
  other arithmetic  1.57 us (7%)
    pallas_call x1, Pallas kernels, on_device(): pl.pallas_call(functools.partial(kernel, (n_mem, n_lat, n_lon, shifts, pa...  19.8 us
    mul x1, other arithmetic, on_device(): return (summed * scale).reshape(1, block, rows)  1.57 us

profile of v4, /device:TPU:0, one launch (start us, length us, event | category | flops | bytes accessed | tf_op | source)
XLA Modules:
  0.0 21.3 jit_solution(6316018482322471550)
XLA Ops:
  0.0 19.8 %shard_map.82 = f32[4,32,256]{2,1,0:T(8,128)} custom-call(bf16[2,16,32,256]{3,2,1,0:T(8,128)(2,1)} %members_hbm.1, bf16[2,16,32,256]{3,2,1,0:T(8,128)(2,1)} %fine_hbm.1, bf16[2,16,16,128]{3,2,1,0:T(8,128)(2,1)} %mid_hbm.1, bf16[2,16,8,64]{3,2,1,0:T(8,128)(2,1)} %coarse_hbm.1, bf16[3,16,16]{2,1,0:T(8,128)(2,1)} %vertical_hbm.1, s32[320]{0:T(512)} %mid_picks_hbm.1, ...), custom_call_target="tpu_custom_call" | custom-call | tf_op jit(solution)/shard_map/pallas_call | solution.py:504
  19.8 1.6 %broadcast_multiply_fusion = f32[4,32,256]{2,1,0:T(8,128)} fusion(f32[4,32,256]{2,1,0:T(8,128)} %shard_map.82), kind=kLoop, calls=%fused_computation | loop fusion | flops 32768 | bytes 262144 | tf_op jit(solution)/shard_map/mul | solution.py:521
